TPU v7x, 32 devices: a whole 2x2x4 slice. The times are simulated.
32 devices in a mesh: prow: 4 (over z), pcol: 8 (over y, x, core).
Axes of the slice: x: 2, y: 2, z: 4, core: 2. Of those that a mesh axis runs over, the one named last changes fastest.
Arguments:
- ainv_in: float32 [36, 4, 18, 8, 128, 128], P(None, 'prow', None, 'pcol'), as said below
- ufactor: bfloat16 [36, 4, 6, 128, 128], P(None, 'prow'), may hold values from -0.08984375 to 0.08984375
- dinv: float32 [6, 128, 128], replicated, may hold values from -6 to 6
- pattern: int32 [144, 144], replicated, may hold values from 0 to 1, as said below
Outputs:
- ainv_out: float32 [36, 4, 18, 8, 128, 128], P(None, 'prow', None, 'pcol')
Inputs may be any that keep to these rules, and one draw needn't show every extreme that they name: For a column j below 6, pattern[i, j] is 0 for i <= j, 1 at the parent row (the nearest row below j that has a 1, at most 3 below j), and the other 1s of column j lie in rows where the parent's column has a 1; for j at least 6, pattern[i, j] is 1 exactly where i > j. `ainv_in`: a symmetric matrix.
All inputs are finite; a program needn't handle non-finite values.
Results may differ from a plain program's by a relative error of at most 0.0003.
Values may be sent and summed in bfloat16 or wider, within the bound.
A program may use at most 192 MiB of HBM per device.

v0:
```python
import jax
import jax.numpy as jnp
from jax import lax
from jax.sharding import PartitionSpec as P


def spread(value, axis, source):
    kept = jnp.where(lax.axis_index(axis) == source, value, 0).astype(value.dtype)
    return lax.psum(kept, axis)


def per_device(ainv_in, ufactor, dinv, pattern):
    row_blocks, _, col_blocks, _, width, _ = ainv_in.shape
    step_count = dinv.shape[0]
    blocks = ainv_in.reshape(row_blocks, col_blocks, width, width)
    lower = ufactor.reshape(row_blocks, step_count, width, width)
    row_count = lax.axis_size("prow")
    col_count = lax.axis_size("pcol")
    prow_id = lax.axis_index("prow")
    pcol_id = lax.axis_index("pcol")
    row_ids = jnp.arange(row_blocks, dtype=jnp.int32) * row_count + prow_id
    col_ids = jnp.arange(col_blocks, dtype=jnp.int32) * col_count + pcol_id
    fold_ratio = col_count // row_count
    pick_slot = pcol_id // row_count
    home_row = pcol_id % row_count
    mask_rows = pattern[row_ids, :]
    live_lower = mask_rows[:, :step_count] > 0
    masked_lower = jnp.where(live_lower[:, :, None, None], lower, jnp.zeros_like(lower))
    chosen_cols = lax.dynamic_index_in_dim(
        masked_lower.reshape(col_blocks, fold_ratio, step_count, width, width),
        pick_slot,
        1,
        keepdims=False,
    )
    other_cols = spread(chosen_cols, "prow", home_row)

    def fetch(column):
        own_col = lax.dynamic_index_in_dim(masked_lower, column, 1, keepdims=False)
        other_rows = lax.dynamic_index_in_dim(other_cols, column, 1, keepdims=False)
        return (own_col, other_rows)

    def advance(taken, matrix):
        column = step_count - 1 - taken
        own_col, other_rows = fetch(column)
        partial_value = -jnp.einsum(
            "acxy,cyz->axz", matrix, other_rows.astype(jnp.float32), precision=lax.Precision.HIGHEST
        )
        col_piece = lax.psum_scatter(partial_value, "pcol", scatter_dimension=1, tiled=True)
        col_whole = lax.all_gather(col_piece, "pcol", axis=1, tiled=True)
        live_rows = lax.dynamic_index_in_dim(mask_rows, column, 1, keepdims=False) > 0
        inverse_col = jnp.where(live_rows[:, None, None], col_whole, jnp.zeros_like(col_whole))
        diag_term = jnp.einsum(
            "axy,axz->yz", own_col.astype(jnp.float32), inverse_col, precision=lax.Precision.HIGHEST
        )
        diag_total = lax.psum(diag_term, "prow")
        diag_block = lax.dynamic_index_in_dim(dinv, column, 0, keepdims=False) - diag_total
        new_col = jnp.where((row_ids == column)[:, None, None], diag_block[None], inverse_col)
        col_slot = column // col_count
        old_col = lax.dynamic_index_in_dim(matrix, col_slot, 1, keepdims=False)
        matrix = lax.dynamic_update_index_in_dim(
            matrix, jnp.where(pcol_id == column % col_count, new_col, old_col), col_slot, 1
        )
        chosen = lax.dynamic_index_in_dim(
            inverse_col.reshape(col_blocks, fold_ratio, width, width), pick_slot, 1, keepdims=False
        )
        across = spread(chosen, "prow", home_row)
        row_vals = jnp.where((col_ids == column)[:, None, None], diag_block[None], across)
        row_vals = jnp.swapaxes(row_vals, 1, 2)
        row_slot = column // row_count
        old_row = lax.dynamic_index_in_dim(matrix, row_slot, 0, keepdims=False)
        matrix = lax.dynamic_update_index_in_dim(
            matrix, jnp.where(prow_id == column % row_count, row_vals, old_row), row_slot, 0
        )
        return matrix

    blocks = lax.fori_loop(0, step_count, advance, blocks)
    return blocks.reshape(ainv_in.shape)


def solution(mesh):
    placed = (
        P(None, "prow", None, "pcol", None, None),
        P(None, "prow", None, None, None),
        P(),
        P(),
    )
    return jax.shard_map(
        per_device,
        mesh=mesh,
        in_specs=placed,
        out_specs=P(None, "prow", None, "pcol", None, None),
        check_vma=False,
    )
```

profile of v0, /device:TPU:17, one launch (start us, length us, event | category | flops | bytes accessed | tf_op | source)
XLA Modules:
  0.0 1239.3 jit_solution(2986418367816600455)
XLA Ops:
  6.5 30.5 %copy.57 = f32[36,1,18,1,128,128]{5,4,3,2,1,0:T(8,128)} copy(f32[36,1,18,1,128,128]{5,4,3,2,1,0:T(8,128)} %param.6) | data formatting | bytes 84934656
  37.8 4.3 fusion.16
  42.2 10.1 copy.31
  52.4 6.5 bitcast_select_fusion.2
  58.9 117.0 %all-reduce.6.cloned.1.call-done = bf16[18,6,128,128]{3,2,1,0:T(8,128)(2,1)} async-done(((bf16[18,6,128,128]{3,2,1,0:T(8,128)(2,1)}), bf16[18,6,128,128]{3,2,1,0:T(8,128)(2,1)}) %all-reduce.6.cloned.1.call-update) | async-done | bytes 3538960 | tf_op jit(solution)/shard_map/psum | solution.py:9
  175.9 1055.9 %while.18 = (s32[]{:T(128)}, f32[36,18,128,128]{3,2,1,0:T(8,128)}, s32[]{:T(128)}, f32[6,128,128]{2,1,0:T(8,128)}, bf16[36,6,128,128]{2,3,0,1:T(8,128)(2,1)}, /*...) while((s32[]{:T(128)}, f32[36,18,128,128]{3,2,1,0:T(8,128)}, ...), condition=%wide.region_5.6_spmd.clone.clone, body=%wide.region_1.5_spmd.clone.clone.sunk | while | flops 17217585152 | bytes 122127656 | solution.py:76
  175.9 27.0 %fusion.30 = f32[36,128,128]{1,2,0:T(8,128)S(1)} fusion(f32[36,18,128,128]{3,2,1,0:T(8,128)} %get-tuple-element.557, bf16[18,6,128,128]{3,2,1,0:T(8,128)(2,1)} %get-tuple-element.586, s32[]{:T(128)S(6)} %select_n.384), kind=kOutput, calls=%fused_computation.6.clone.1 | convolution fusion | flops 16308043776 | bytes 45416452 | tf_op jit(solution)/shard_map/while/body/eval_jaxpr/acxy,cyz->axz/dot_general | solution.py:45
  202.9 2.3 copy.41
  205.3 43.6 %reduce-scatter.2.cloned.1.call-done = f32[36,16,128]{2,0,1:T(8,128)} async-done(((f32[36,128,128]{2,0,1:T(8,128)}), f32[36,16,128]{2,0,1:T(8,128)}) %reduce-scatter.2.cloned.1.call-update) | async-done | bytes 294928 | tf_op jit(solution)/shard_map/while/body/eval_jaxpr/reduce_scatter | solution.py:48
  248.9 1.7 copy.42
  250.8 29.9 %all-gather.2.cloned.1.call-done = f32[36,128,128]{2,1,0:T(8,128)} async-done(((f32[36,16,128]{2,1,0:T(8,128)}), f32[36,128,128]{2,1,0:T(8,128)}) %all-gather.2.cloned.1.call-update) | async-done | bytes 2359312 | tf_op jit(solution)/shard_map/while/body/eval_jaxpr/all_gather | solution.py:49
  280.7 1.9 broadcast_select_fusion.2
  282.6 3.3 fusion.31
  287.6 3.5 constant_dynamic-slice_fusion.8
  291.0 53.6 %all-reduce.8.cloned.1.call-done = (f32[128,128]{1,0:T(8,128)}, f32[18,128,128]{1,2,0:T(8,128)}) async-done(((f32[128,128]{1,0:T(8,128)}, f32[18,128,128]{1,2,0:T(8,128)}), (f32[128,128]{1,0:T(8,128)}, f32[18,128,128]{1,2,0:T(8,128)})) %all-reduce.8.cloned.1.call-update) | async-done | bytes 1245200 | tf_op jit(solution)/shard_map/while/body/eval_jaxpr/psum | solution.py:55
  345.6 3.5 bitcast_dynamic-update-slice_fusion.4
  351.9 27.0 %fusion.30 = f32[36,128,128]{1,2,0:T(8,128)S(1)} fusion(f32[36,18,128,128]{3,2,1,0:T(8,128)} %get-tuple-element.557, bf16[18,6,128,128]{3,2,1,0:T(8,128)(2,1)} %get-tuple-element.586, s32[]{:T(128)S(6)} %select_n.384), kind=kOutput, calls=%fused_computation.6.clone.1 | convolution fusion | flops 16308043776 | bytes 45416452 | tf_op jit(solution)/shard_map/while/body/eval_jaxpr/acxy,cyz->axz/dot_general | solution.py:45
  378.9 2.3 copy.41
  381.3 43.6 %reduce-scatter.2.cloned.1.call-done = f32[36,16,128]{2,0,1:T(8,128)} async-done(((f32[36,128,128]{2,0,1:T(8,128)}), f32[36,16,128]{2,0,1:T(8,128)}) %reduce-scatter.2.cloned.1.call-update) | async-done | bytes 294928 | tf_op jit(solution)/shard_map/while/body/eval_jaxpr/reduce_scatter | solution.py:48
  424.9 1.7 copy.42
  426.8 29.9 %all-gather.2.cloned.1.call-done = f32[36,128,128]{2,1,0:T(8,128)} async-done(((f32[36,16,128]{2,1,0:T(8,128)}), f32[36,128,128]{2,1,0:T(8,128)}) %all-gather.2.cloned.1.call-update) | async-done | bytes 2359312 | tf_op jit(solution)/shard_map/while/body/eval_jaxpr/all_gather | solution.py:49
  456.7 1.9 broadcast_select_fusion.2
  458.6 3.3 fusion.31
  463.6 3.5 constant_dynamic-slice_fusion.8
  467.0 53.6 %all-reduce.8.cloned.1.call-done = (f32[128,128]{1,0:T(8,128)}, f32[18,128,128]{1,2,0:T(8,128)}) async-done(((f32[128,128]{1,0:T(8,128)}, f32[18,128,128]{1,2,0:T(8,128)}), (f32[128,128]{1,0:T(8,128)}, f32[18,128,128]{1,2,0:T(8,128)})) %all-reduce.8.cloned.1.call-update) | async-done | bytes 1245200 | tf_op jit(solution)/shard_map/while/body/eval_jaxpr/psum | solution.py:55
  521.6 3.5 bitcast_dynamic-update-slice_fusion.4
  527.9 27.1 %fusion.30 = f32[36,128,128]{1,2,0:T(8,128)S(1)} fusion(f32[36,18,128,128]{3,2,1,0:T(8,128)} %get-tuple-element.557, bf16[18,6,128,128]{3,2,1,0:T(8,128)(2,1)} %get-tuple-element.586, s32[]{:T(128)S(6)} %select_n.384), kind=kOutput, calls=%fused_computation.6.clone.1 | convolution fusion | flops 16308043776 | bytes 45416452 | tf_op jit(solution)/shard_map/while/body/eval_jaxpr/acxy,cyz->axz/dot_general | solution.py:45
  555.0 2.3 copy.41
  557.3 43.6 %reduce-scatter.2.cloned.1.call-done = f32[36,16,128]{2,0,1:T(8,128)} async-done(((f32[36,128,128]{2,0,1:T(8,128)}), f32[36,16,128]{2,0,1:T(8,128)}) %reduce-scatter.2.cloned.1.call-update) | async-done | bytes 294928 | tf_op jit(solution)/shard_map/while/body/eval_jaxpr/reduce_scatter | solution.py:48
  600.9 1.7 copy.42
  602.8 29.9 %all-gather.2.cloned.1.call-done = f32[36,128,128]{2,1,0:T(8,128)} async-done(((f32[36,16,128]{2,1,0:T(8,128)}), f32[36,128,128]{2,1,0:T(8,128)}) %all-gather.2.cloned.1.call-update) | async-done | bytes 2359312 | tf_op jit(solution)/shard_map/while/body/eval_jaxpr/all_gather | solution.py:49
  632.7 1.9 broadcast_select_fusion.2
  634.6 3.3 fusion.31
  639.6 3.5 constant_dynamic-slice_fusion.8
  643.0 53.6 %all-reduce.8.cloned.1.call-done = (f32[128,128]{1,0:T(8,128)}, f32[18,128,128]{1,2,0:T(8,128)}) async-done(((f32[128,128]{1,0:T(8,128)}, f32[18,128,128]{1,2,0:T(8,128)}), (f32[128,128]{1,0:T(8,128)}, f32[18,128,128]{1,2,0:T(8,128)})) %all-reduce.8.cloned.1.call-update) | async-done | bytes 1245200 | tf_op jit(solution)/shard_map/while/body/eval_jaxpr/psum | solution.py:55
  697.6 3.5 bitcast_dynamic-update-slice_fusion.4
  703.9 27.0 %fusion.30 = f32[36,128,128]{1,2,0:T(8,128)S(1)} fusion(f32[36,18,128,128]{3,2,1,0:T(8,128)} %get-tuple-element.557, bf16[18,6,128,128]{3,2,1,0:T(8,128)(2,1)} %get-tuple-element.586, s32[]{:T(128)S(6)} %select_n.384), kind=kOutput, calls=%fused_computation.6.clone.1 | convolution fusion | flops 16308043776 | bytes 45416452 | tf_op jit(solution)/shard_map/while/body/eval_jaxpr/acxy,cyz->axz/dot_general | solution.py:45
  730.9 2.3 copy.41
  733.3 43.6 %reduce-scatter.2.cloned.1.call-done = f32[36,16,128]{2,0,1:T(8,128)} async-done(((f32[36,128,128]{2,0,1:T(8,128)}), f32[36,16,128]{2,0,1:T(8,128)}) %reduce-scatter.2.cloned.1.call-update) | async-done | bytes 294928 | tf_op jit(solution)/shard_map/while/body/eval_jaxpr/reduce_scatter | solution.py:48
  776.9 1.7 copy.42
  778.7 29.9 %all-gather.2.cloned.1.call-done = f32[36,128,128]{2,1,0:T(8,128)} async-done(((f32[36,16,128]{2,1,0:T(8,128)}), f32[36,128,128]{2,1,0:T(8,128)}) %all-gather.2.cloned.1.call-update) | async-done | bytes 2359312 | tf_op jit(solution)/shard_map/while/body/eval_jaxpr/all_gather | solution.py:49
  808.6 1.9 broadcast_select_fusion.2
  810.5 3.3 fusion.31
  815.5 3.5 constant_dynamic-slice_fusion.8
  819.0 53.6 %all-reduce.8.cloned.1.call-done = (f32[128,128]{1,0:T(8,128)}, f32[18,128,128]{1,2,0:T(8,128)}) async-done(((f32[128,128]{1,0:T(8,128)}, f32[18,128,128]{1,2,0:T(8,128)}), (f32[128,128]{1,0:T(8,128)}, f32[18,128,128]{1,2,0:T(8,128)})) %all-reduce.8.cloned.1.call-update) | async-done | bytes 1245200 | tf_op jit(solution)/shard_map/while/body/eval_jaxpr/psum | solution.py:55
  873.6 3.5 bitcast_dynamic-update-slice_fusion.4
  879.9 27.0 %fusion.30 = f32[36,128,128]{1,2,0:T(8,128)S(1)} fusion(f32[36,18,128,128]{3,2,1,0:T(8,128)} %get-tuple-element.557, bf16[18,6,128,128]{3,2,1,0:T(8,128)(2,1)} %get-tuple-element.586, s32[]{:T(128)S(6)} %select_n.384), kind=kOutput, calls=%fused_computation.6.clone.1 | convolution fusion | flops 16308043776 | bytes 45416452 | tf_op jit(solution)/shard_map/while/body/eval_jaxpr/acxy,cyz->axz/dot_general | solution.py:45
  906.9 2.3 copy.41
  909.3 43.6 %reduce-scatter.2.cloned.1.call-done = f32[36,16,128]{2,0,1:T(8,128)} async-done(((f32[36,128,128]{2,0,1:T(8,128)}), f32[36,16,128]{2,0,1:T(8,128)}) %reduce-scatter.2.cloned.1.call-update) | async-done | bytes 294928 | tf_op jit(solution)/shard_map/while/body/eval_jaxpr/reduce_scatter | solution.py:48
  954.7 29.9 %all-gather.2.cloned.1.call-done = f32[36,128,128]{2,1,0:T(8,128)} async-done(((f32[36,16,128]{2,1,0:T(8,128)}), f32[36,128,128]{2,1,0:T(8,128)}) %all-gather.2.cloned.1.call-update) | async-done | bytes 2359312 | tf_op jit(solution)/shard_map/while/body/eval_jaxpr/all_gather | solution.py:49
  984.6 1.9 broadcast_select_fusion.2
  986.5 3.3 fusion.31
  991.5 3.5 constant_dynamic-slice_fusion.8
  995.0 53.6 %all-reduce.8.cloned.1.call-done = (f32[128,128]{1,0:T(8,128)}, f32[18,128,128]{1,2,0:T(8,128)}) async-done(((f32[128,128]{1,0:T(8,128)}, f32[18,128,128]{1,2,0:T(8,128)}), (f32[128,128]{1,0:T(8,128)}, f32[18,128,128]{1,2,0:T(8,128)})) %all-reduce.8.cloned.1.call-update) | async-done | bytes 1245200 | tf_op jit(solution)/shard_map/while/body/eval_jaxpr/psum | solution.py:55
  1049.5 3.5 bitcast_dynamic-update-slice_fusion.4
  1055.9 27.0 %fusion.30 = f32[36,128,128]{1,2,0:T(8,128)S(1)} fusion(f32[36,18,128,128]{3,2,1,0:T(8,128)} %get-tuple-element.557, bf16[18,6,128,128]{3,2,1,0:T(8,128)(2,1)} %get-tuple-element.586, s32[]{:T(128)S(6)} %select_n.384), kind=kOutput, calls=%fused_computation.6.clone.1 | convolution fusion | flops 16308043776 | bytes 45416452 | tf_op jit(solution)/shard_map/while/body/eval_jaxpr/acxy,cyz->axz/dot_general | solution.py:45
  1082.9 2.3 copy.41
  1085.2 43.6 %reduce-scatter.2.cloned.1.call-done = f32[36,16,128]{2,0,1:T(8,128)} async-done(((f32[36,128,128]{2,0,1:T(8,128)}), f32[36,16,128]{2,0,1:T(8,128)}) %reduce-scatter.2.cloned.1.call-update) | async-done | bytes 294928 | tf_op jit(solution)/shard_map/while/body/eval_jaxpr/reduce_scatter | solution.py:48
  1130.7 29.9 %all-gather.2.cloned.1.call-done = f32[36,128,128]{2,1,0:T(8,128)} async-done(((f32[36,16,128]{2,1,0:T(8,128)}), f32[36,128,128]{2,1,0:T(8,128)}) %all-gather.2.cloned.1.call-update) | async-done | bytes 2359312 | tf_op jit(solution)/shard_map/while/body/eval_jaxpr/all_gather | solution.py:49
  1160.6 1.9 broadcast_select_fusion.2
  1162.5 3.3 fusion.31
  1167.5 3.5 constant_dynamic-slice_fusion.8
  1170.9 53.6 %all-reduce.8.cloned.1.call-done = (f32[128,128]{1,0:T(8,128)}, f32[18,128,128]{1,2,0:T(8,128)}) async-done(((f32[128,128]{1,0:T(8,128)}, f32[18,128,128]{1,2,0:T(8,128)}), (f32[128,128]{1,0:T(8,128)}, f32[18,128,128]{1,2,0:T(8,128)})) %all-reduce.8.cloned.1.call-update) | async-done | bytes 1245200 | tf_op jit(solution)/shard_map/while/body/eval_jaxpr/psum | solution.py:55
  1225.5 3.5 bitcast_dynamic-update-slice_fusion.4
  (136 shorter events, 38.4 us)
Async XLA Ops:
  6.5 30.6 %copy-start = (s32[144,144]{1,0:T(8,128)S(1)}, s32[144,144]{1,0:T(8,128)}, u32[]{:S(2)}) copy-start(s32[144,144]{1,0:T(8,128)} %param.9) | copy-start | bytes 248836
  6.5 169.4 %all-reduce.6.cloned.1.call-start = ((), (), s32[]{:S(2)}) async-start(), calls=%async_computation.1 | async-start | bytes 7077888 | tf_op jit(solution)/shard_map/psum | solution.py:9
  175.9 73.0 %reduce-scatter.2.cloned.1.call-start = ((), (), s32[]{:S(2)}) async-start(), calls=%async_computation.2 | async-start | bytes 2949120 | tf_op jit(solution)/shard_map/while/body/eval_jaxpr/reduce_scatter | solution.py:48
  205.3 75.4 %all-gather.2.cloned.1.call-start = ((), (), s32[]{:S(2)}) async-start(), calls=%async_computation.3 | async-start | bytes 2654208 | tf_op jit(solution)/shard_map/while/body/eval_jaxpr/all_gather | solution.py:49
  250.7 93.9 %all-reduce.8.cloned.1.call-start = ((), (), s32[]{:S(2)}) async-start(), calls=%async_computation.4 | async-start | bytes 2490368 | tf_op jit(solution)/shard_map/while/body/eval_jaxpr/psum | solution.py:55
  287.6 58.0 %copy-start.2 = (f32[36,128,128]{2,1,0:T(8,128)S(1)}, f32[36,128,128]{2,1,0:T(8,128)}, u32[]{:S(2)}) copy-start(f32[36,128,128]{2,1,0:T(8,128)} %all-gather.2.cloned.1.call-done) | copy-start | bytes 7077892 | tf_op jit(solution)/shard_map/while
  349.1 1.6 copy-start.3
  351.9 73.0 %reduce-scatter.2.cloned.1.call-start = ((), (), s32[]{:S(2)}) async-start(), calls=%async_computation.2 | async-start | bytes 2949120 | tf_op jit(solution)/shard_map/while/body/eval_jaxpr/reduce_scatter | solution.py:48
  381.2 75.4 %all-gather.2.cloned.1.call-start = ((), (), s32[]{:S(2)}) async-start(), calls=%async_computation.3 | async-start | bytes 2654208 | tf_op jit(solution)/shard_map/while/body/eval_jaxpr/all_gather | solution.py:49
  426.7 93.9 %all-reduce.8.cloned.1.call-start = ((), (), s32[]{:S(2)}) async-start(), calls=%async_computation.4 | async-start | bytes 2490368 | tf_op jit(solution)/shard_map/while/body/eval_jaxpr/psum | solution.py:55
  463.5 58.0 %copy-start.2 = (f32[36,128,128]{2,1,0:T(8,128)S(1)}, f32[36,128,128]{2,1,0:T(8,128)}, u32[]{:S(2)}) copy-start(f32[36,128,128]{2,1,0:T(8,128)} %all-gather.2.cloned.1.call-done) | copy-start | bytes 7077892 | tf_op jit(solution)/shard_map/while
  525.1 1.6 copy-start.3
  527.9 73.0 %reduce-scatter.2.cloned.1.call-start = ((), (), s32[]{:S(2)}) async-start(), calls=%async_computation.2 | async-start | bytes 2949120 | tf_op jit(solution)/shard_map/while/body/eval_jaxpr/reduce_scatter | solution.py:48
  557.3 75.4 %all-gather.2.cloned.1.call-start = ((), (), s32[]{:S(2)}) async-start(), calls=%async_computation.3 | async-start | bytes 2654208 | tf_op jit(solution)/shard_map/while/body/eval_jaxpr/all_gather | solution.py:49
  602.7 93.9 %all-reduce.8.cloned.1.call-start = ((), (), s32[]{:S(2)}) async-start(), calls=%async_computation.4 | async-start | bytes 2490368 | tf_op jit(solution)/shard_map/while/body/eval_jaxpr/psum | solution.py:55
  639.6 58.0 %copy-start.2 = (f32[36,128,128]{2,1,0:T(8,128)S(1)}, f32[36,128,128]{2,1,0:T(8,128)}, u32[]{:S(2)}) copy-start(f32[36,128,128]{2,1,0:T(8,128)} %all-gather.2.cloned.1.call-done) | copy-start | bytes 7077892 | tf_op jit(solution)/shard_map/while
  701.1 1.6 copy-start.3
  703.9 73.0 %reduce-scatter.2.cloned.1.call-start = ((), (), s32[]{:S(2)}) async-start(), calls=%async_computation.2 | async-start | bytes 2949120 | tf_op jit(solution)/shard_map/while/body/eval_jaxpr/reduce_scatter | solution.py:48
  733.2 75.4 %all-gather.2.cloned.1.call-start = ((), (), s32[]{:S(2)}) async-start(), calls=%async_computation.3 | async-start | bytes 2654208 | tf_op jit(solution)/shard_map/while/body/eval_jaxpr/all_gather | solution.py:49
  778.6 93.9 %all-reduce.8.cloned.1.call-start = ((), (), s32[]{:S(2)}) async-start(), calls=%async_computation.4 | async-start | bytes 2490368 | tf_op jit(solution)/shard_map/while/body/eval_jaxpr/psum | solution.py:55
  815.5 58.0 %copy-start.2 = (f32[36,128,128]{2,1,0:T(8,128)S(1)}, f32[36,128,128]{2,1,0:T(8,128)}, u32[]{:S(2)}) copy-start(f32[36,128,128]{2,1,0:T(8,128)} %all-gather.2.cloned.1.call-done) | copy-start | bytes 7077892 | tf_op jit(solution)/shard_map/while
  877.0 1.6 copy-start.3
  879.9 73.0 %reduce-scatter.2.cloned.1.call-start = ((), (), s32[]{:S(2)}) async-start(), calls=%async_computation.2 | async-start | bytes 2949120 | tf_op jit(solution)/shard_map/while/body/eval_jaxpr/reduce_scatter | solution.py:48
  909.2 75.4 %all-gather.2.cloned.1.call-start = ((), (), s32[]{:S(2)}) async-start(), calls=%async_computation.3 | async-start | bytes 2654208 | tf_op jit(solution)/shard_map/while/body/eval_jaxpr/all_gather | solution.py:49
  954.6 93.9 %all-reduce.8.cloned.1.call-start = ((), (), s32[]{:S(2)}) async-start(), calls=%async_computation.4 | async-start | bytes 2490368 | tf_op jit(solution)/shard_map/while/body/eval_jaxpr/psum | solution.py:55
  991.5 58.0 %copy-start.2 = (f32[36,128,128]{2,1,0:T(8,128)S(1)}, f32[36,128,128]{2,1,0:T(8,128)}, u32[]{:S(2)}) copy-start(f32[36,128,128]{2,1,0:T(8,128)} %all-gather.2.cloned.1.call-done) | copy-start | bytes 7077892 | tf_op jit(solution)/shard_map/while
  1053.0 1.6 copy-start.3
  1055.8 73.0 %reduce-scatter.2.cloned.1.call-start = ((), (), s32[]{:S(2)}) async-start(), calls=%async_computation.2 | async-start | bytes 2949120 | tf_op jit(solution)/shard_map/while/body/eval_jaxpr/reduce_scatter | solution.py:48
  1085.2 75.4 %all-gather.2.cloned.1.call-start = ((), (), s32[]{:S(2)}) async-start(), calls=%async_computation.3 | async-start | bytes 2654208 | tf_op jit(solution)/shard_map/while/body/eval_jaxpr/all_gather | solution.py:49
  1130.6 93.9 %all-reduce.8.cloned.1.call-start = ((), (), s32[]{:S(2)}) async-start(), calls=%async_computation.4 | async-start | bytes 2490368 | tf_op jit(solution)/shard_map/while/body/eval_jaxpr/psum | solution.py:55
  1167.5 58.0 %copy-start.2 = (f32[36,128,128]{2,1,0:T(8,128)S(1)}, f32[36,128,128]{2,1,0:T(8,128)}, u32[]{:S(2)}) copy-start(f32[36,128,128]{2,1,0:T(8,128)} %all-gather.2.cloned.1.call-done) | copy-start | bytes 7077892 | tf_op jit(solution)/shard_map/while
  1229.0 1.6 copy-start.3
  1231.8 0.9 copy-start.1
Sparse Core Ops, SparseCore 0:
  42.2 133.6 all-reduce.5
  205.4 43.4 reduce-scatter.1
  250.8 29.8 all-gather.1
  287.6 56.9 all-reduce.7
  381.4 43.4 reduce-scatter.1
  426.8 29.8 all-gather.1
  463.6 56.9 all-reduce.7
  557.4 43.4 reduce-scatter.1
  602.8 29.8 all-gather.1
  639.6 56.9 all-reduce.7
  733.4 43.4 reduce-scatter.1
  778.8 29.8 all-gather.1
  815.6 56.9 all-reduce.7
  909.3 43.4 reduce-scatter.1
  954.7 29.8 all-gather.1
  991.5 56.9 all-reduce.7
  1085.3 43.4 reduce-scatter.1
  1130.7 29.8 all-gather.1
  1167.5 56.9 all-reduce.7
where the time goes:
time: 1240 us
  waiting for transfers between devices  880 us (71%)
  matrix products  182 us (15%)
  local copies, waits for them, and re-layouts  100 us (8%)
  other arithmetic  62.3 us (5%)
  between operations  13.1 us (1%)
    psum x6, waiting for transfers between devices, advance(): diag_total = lax.psum(diag_term, 'prow')  321 us
    reduce_scatter x6, waiting for transfers between devices, advance(): lax.psum_scatter(partial_value, 'pcol', scatter_dimension=1, tiled=True)  262 us
    all_gather x6, waiting for transfers between devices, advance(): col_whole = lax.all_gather(col_piece, 'pcol', axis=1, tiled=True)  179 us
    dot_general x6, matrix products, advance(): jnp.einsum('acxy,cyz->axz', matrix, other_rows.astype(jnp.float32), preci...  162 us
    psum x1, waiting for transfers between devices, spread(): return lax.psum(kept, axis)  117 us
    unnamed x7, local copies, waits for them, and re-layouts  41.6 us
  transfers between devices with their start and end apart: 19, of which 19 were waited for; matrix products, arithmetic and copies ran while one was open for 3% of the time, Pallas kernels for 0%

commit v1 on v0

v1 whole, which is shorter than its diff:
```python
import functools

import jax
import jax.numpy as jnp
from jax import lax
from jax.experimental import pallas as pl
from jax.experimental.pallas import tpu as pltpu
from jax.sharding import PartitionSpec as P

F32 = jnp.float32
BF16 = jnp.bfloat16


def largest_divisor(value, most):
    return max(d for d in range(1, most + 1) if value % d == 0)


def pieces(value, count):
    parts = []
    for _ in range(count):
        part = value.astype(BF16)
        parts.append(part)
        value = value - part.astype(F32)
    return parts


def mixed_dot(left, right, dims=(((1,), (0,)), ((), ())), count=3):
    total = None
    for part in reversed(pieces(left, count)):
        term = lax.dot_general(part, right, dims, preferred_element_type=F32)
        total = term if total is None else total + term
    return total


def product_kernel(x_ref, u_ref, o_ref, y_ref, acc_ref):
    k = pl.program_id(1)
    tall, group, width, _ = x_ref.shape
    o_ref[...] = x_ref[...]
    tile = jnp.concatenate([x_ref[:, g].reshape(tall * width, width) for g in range(group)], axis=1)
    high, low = pieces(tile, 2)
    left = u_ref[k]
    part = jnp.dot(left, low, preferred_element_type=F32) + jnp.dot(left, high, preferred_element_type=F32)

    @pl.when(k == 0)
    def _():
        acc_ref[...] = part

    @pl.when(k > 0)
    def _():
        acc_ref[...] += part

    @pl.when(k == pl.num_programs(1) - 1)
    def _():
        y_ref[...] = acc_ref[...].T


def product(blocks, masked, width, steps):
    row_blocks, col_blocks = blocks.shape[:2]
    group = 2 if col_blocks % 2 == 0 else 1
    tall = largest_divisor(row_blocks, 9)
    chunks = row_blocks // tall
    left = masked.reshape(chunks, tall, steps, width, width).transpose(0, 2, 4, 1, 3)
    left = left.reshape(chunks, steps * width, tall * width)
    return pl.pallas_call(
        product_kernel,
        grid=(col_blocks // group, chunks),
        in_specs=[
            pl.BlockSpec((tall, group, width, width), lambda c, k: (k, c, 0, 0)),
            pl.BlockSpec(left.shape, lambda c, k: (0, 0, 0), pipeline_mode=pl.Buffered(1)),
        ],
        out_specs=[
            pl.BlockSpec((tall, group, width, width), lambda c, k: (k, c, 0, 0)),
            pl.BlockSpec((group * width, steps * width), lambda c, k: (c, 0)),
        ],
        out_shape=[
            jax.ShapeDtypeStruct(blocks.shape, F32),
            jax.ShapeDtypeStruct((col_blocks * width, steps * width), F32),
        ],
        scratch_shapes=[pltpu.VMEM((steps * width, group * width), F32)],
        compiler_params=pltpu.CompilerParams(vmem_limit_bytes=56 << 20),
        cost_estimate=pl.CostEstimate(
            flops=4 * row_blocks * col_blocks * width**3 * steps,
            bytes_accessed=8 * row_blocks * col_blocks * width**2,
            transcendentals=0,
        ),
    )(blocks, left)


def substitute_kernel(steps, y_ref, mask_ref, small_ref, rows_ref, z_ref, p_ref):
    width = y_ref.shape[1] // steps
    for k in reversed(range(steps)):
        here = slice(k * width, (k + 1) * width)
        value = y_ref[:, here]
        if k + 1 < steps:
            later = slice((k + 1) * width, steps * width)
            value = value + mixed_dot(z_ref[:, later], small_ref[later, here])
        z_ref[:, here] = jnp.where(mask_ref[:, k : k + 1] > 0, -value, 0.0)
    for j in range(steps):
        upto = slice(0, (j + 1) * width)
        there = slice(j * width, (j + 1) * width)
        if j + 1 < steps:
            p_ref[there, (j + 1) * width :] = jnp.zeros((width, (steps - j - 1) * width), F32)
        p_ref[there, upto] = mixed_dot(z_ref[:, there], rows_ref[:, upto], (((0,), (0,)), ((), ())))


def corner_kernel(steps, p_ref, small_ref, dinv_ref, mask_ref, s_ref):
    width = dinv_ref.shape[1]
    for k in reversed(range(steps)):
        here = slice(k * width, (k + 1) * width)
        diag = dinv_ref[k] - p_ref[here, here].T
        if k + 1 < steps:
            later = slice((k + 1) * width, steps * width)
            factor = small_ref[later, here]
            value = p_ref[later, here] + mixed_dot(s_ref[later, later], factor)
            value = jnp.where(mask_ref[later, k : k + 1] > 0, -value, 0.0)
            diag = diag - mixed_dot(value, factor, (((0,), (0,)), ((), ()))).T
            s_ref[later, here] = value
            s_ref[here, later] = value.T
        s_ref[here, here] = diag.T


def per_device(ainv_in, ufactor, dinv, pattern):
    row_blocks, _, col_blocks, _, width, _ = ainv_in.shape
    steps = dinv.shape[0]
    blocks = ainv_in.reshape(row_blocks, col_blocks, width, width)
    lower = ufactor.reshape(row_blocks, steps, width, width)
    row_count = lax.axis_size("prow")
    col_count = lax.axis_size("pcol")
    prow_id = lax.axis_index("prow")
    pcol_id = lax.axis_index("pcol")
    fold = col_count // row_count
    slots = -(-steps // row_count)
    assert slots <= fold and steps <= col_count
    row_ids = jnp.arange(row_blocks, dtype=jnp.int32) * row_count + prow_id
    col_ids = jnp.arange(col_blocks, dtype=jnp.int32) * col_count + pcol_id

    live = pattern[row_ids, :steps] > 0
    masked = jnp.where(live[:, :, None, None], lower, jnp.zeros_like(lower))
    outer = jnp.where((row_ids >= steps)[:, None, None, None], masked, jnp.zeros_like(masked))

    copied, partial_y = product(blocks, outer, width, steps)

    small = lax.all_gather(masked[:slots], "prow", axis=1)
    small = small.reshape(slots * row_count, steps, width, width)[:steps]
    small = small.transpose(0, 2, 1, 3).reshape(steps * width, steps * width)

    chosen = lax.dynamic_index_in_dim(
        outer.reshape(col_blocks, fold, steps, width, width), pcol_id // row_count, 1, keepdims=False
    )
    chosen = chosen.transpose(0, 2, 1, 3).reshape(col_blocks * width, steps * width)
    chosen = jnp.where(prow_id == pcol_id % row_count, chosen, jnp.zeros_like(chosen))
    factor_rows = lax.psum_scatter(chosen, "prow", scatter_dimension=0, tiled=True)

    share_y = lax.psum_scatter(partial_y, "prow", scatter_dimension=0, tiled=True)
    share = share_y.shape[0]
    mask_cols = jnp.where((col_ids >= steps)[:, None], pattern[col_ids, :steps], 0).astype(F32)
    mask_rows = lax.dynamic_slice_in_dim(jnp.repeat(mask_cols, width, axis=0), prow_id * share, share, 0)

    params = pltpu.CompilerParams(vmem_limit_bytes=40 << 20)
    share_z, products = pl.pallas_call(
        functools.partial(substitute_kernel, steps),
        out_shape=[
            jax.ShapeDtypeStruct(share_y.shape, F32),
            jax.ShapeDtypeStruct((steps * width, steps * width), F32),
        ],
        compiler_params=params,
    )(share_y, mask_rows, small, factor_rows)
    products = lax.psum(products, ("prow", "pcol"))

    mask_small = jnp.repeat(pattern[:steps, :steps].astype(F32), width, axis=0)
    corner = pl.pallas_call(
        functools.partial(corner_kernel, steps),
        out_shape=jax.ShapeDtypeStruct((steps * width, steps * width), F32),
        compiler_params=params,
    )(products, small, dinv, mask_small)
    corner = corner.reshape(steps, width, steps, width)

    padded = jnp.pad(share_z, ((0, 0), (0, (slots * row_count - steps) * width)))
    padded = padded.reshape(share, slots, row_count, width)
    mine = lax.all_to_all(padded, "prow", split_axis=2, concat_axis=0, tiled=True)
    mine = mine.reshape(col_blocks, width, slots, width)

    received = []
    for turn in range(fold):
        pairs = []
        for slot in range(slots):
            side = (turn + slot) % fold
            for p in range(row_count):
                if slot * row_count + p < steps:
                    for r in range(row_count):
                        source = p * col_count + side * row_count + r
                        target = r * col_count + slot * row_count + p
                        pairs.append((source, target))
        slot = jnp.minimum((pcol_id // row_count + fold - turn) % fold, slots - 1)
        payload = lax.dynamic_index_in_dim(mine, slot, 2, keepdims=False)
        received.append(lax.ppermute(payload, ("prow", "pcol"), pairs))
    my_slot = pcol_id // row_count
    stacked = jnp.stack(received)
    new_col = jnp.stack([stacked[(side - my_slot) % fold] for side in range(fold)], axis=1)
    new_col = new_col.reshape(row_blocks, width, width)
    own = jnp.minimum(pcol_id, steps - 1)
    corner_col = lax.dynamic_index_in_dim(corner, own, 2, keepdims=False)
    for slot in range(slots):
        index = slot * row_count + prow_id
        block = lax.dynamic_index_in_dim(corner_col, jnp.minimum(index, steps - 1), 0, keepdims=False)
        new_col = new_col.at[slot].set(jnp.where(index < steps, block, new_col[slot]))
    old_col = copied[:, 0]
    matrix = copied.at[:, 0].set(jnp.where(pcol_id < steps, new_col, old_col))
    for slot in range(slots):
        index = slot * row_count + prow_id
        new_row = jnp.swapaxes(mine[:, :, slot], 1, 2)
        block = lax.dynamic_index_in_dim(corner, jnp.minimum(index, steps - 1), 0, keepdims=False)
        block = lax.dynamic_index_in_dim(block, own, 1, keepdims=False)
        new_row = new_row.at[0].set(jnp.where(pcol_id < steps, block, new_row[0]))
        matrix = matrix.at[slot].set(jnp.where(index < steps, new_row, matrix[slot]))
    return matrix.reshape(ainv_in.shape)


def solution(mesh):
    placed = (
        P(None, "prow", None, "pcol", None, None),
        P(None, "prow", None, None, None),
        P(),
        P(),
    )
    return jax.shard_map(
        per_device,
        mesh=mesh,
        in_specs=placed,
        out_specs=P(None, "prow", None, "pcol", None, None),
        check_vma=False,
    )
```

time: 1240 us -> 647 us (0.52)
  waiting for transfers between devices: 880 us -> 245 us
  matrix products: 182 us -> 0 us
  local copies, waits for them, and re-layouts: 100 us -> 264 us
  Pallas kernels: 0 us -> 74.3 us
  other arithmetic: 62.3 us -> 28 us
    psum x7 -> x1, waiting for transfers between devices: 438 us -> 111 us  [per_device(): products = lax.psum(products, ('prow', 'pcol'))]
    reduce_scatter x6 -> x2, waiting for transfers between devices: 262 us -> 72.7 us  [the longest x1 72.7 us: per_device(): lax.psum_scatter(partial_y, 'prow', scatter_dimension=0, tiled=True)]
    dot_general x12 -> x0, matrix products: 182 us -> none  [the longest x6 162 us: advance(): jnp.einsum('acxy,cyz->axz', matrix, other_rows.astype(jnp.float32), preci...]
    all_gather x6 -> x1, waiting for transfers between devices: 179 us -> 0.02 us  [per_device(): small = lax.all_gather(masked[:slots], 'prow', axis=1)]
    gather x1 -> x216, local copies, waits for them, and re-layouts: 0.61 us -> 151 us  [per_device(): mask_rows = pattern[row_ids, :]]
    pallas_call x0 -> x3, Pallas kernels: none -> 74.3 us  [the longest x1 63.9 us: product(): pl.pallas_call(product_kernel, grid=(col_blocks // group, chunks), in_spe...]
    all_to_all x0 -> x1, waiting for transfers between devices: none -> 60.9 us  [per_device(): lax.all_to_all(padded, 'prow', split_axis=2, concat_axis=0, tiled=True)]
    reshape x0 -> x5, local copies, waits for them, and re-layouts: none -> 33.5 us  [the longest x2 25.9 us: product(): left = left.reshape(chunks, steps * width, tall * width)]
  transfers between devices with their start and end apart: 19 -> 7, of which waited for: 19 -> 3; matrix products, arithmetic and copies ran while one was open for 3% -> 22% of each run, Pallas kernels for 0% -> 11%
where the time goes in v1:
time: 647 us; the launch traced here: 636 us
  local copies, waits for them, and re-layouts  264 us (41%)
  waiting for transfers between devices  245 us (38%)
  Pallas kernels  74.3 us (11%)
  other arithmetic  28 us (4%)
  between operations  13.6 us (2%)
  starting transfers between devices  11.1 us (2%)
    gather x216, local copies, waits for them, and re-layouts  151 us
    psum x1, waiting for transfers between devices, per_device(): products = lax.psum(products, ('prow', 'pcol'))  111 us
    reduce_scatter x1, waiting for transfers between devices, per_device(): lax.psum_scatter(partial_y, 'prow', scatter_dimension=0, tiled=True)  72.7 us
    pallas_call x1, Pallas kernels, product(): pl.pallas_call(product_kernel, grid=(col_blocks // group, chunks), in_spe...  63.9 us
    all_to_all x1, waiting for transfers between devices, per_device(): lax.all_to_all(padded, 'prow', split_axis=2, concat_axis=0, tiled=True)  60.9 us
    unnamed x24, local copies, waits for them, and re-layouts  39.2 us
    pallas_call x1, local copies, waits for them, and re-layouts, product(): pl.pallas_call(product_kernel, grid=(col_blocks // group, chunks), in_spe...  30.8 us
    reshape x2, local copies, waits for them, and re-layouts, product(): left = left.reshape(chunks, steps * width, tall * width)  25.9 us
  transfers between devices with their start and end apart: 7, of which 3 were waited for; matrix products, arithmetic and copies ran while one was open for 22% of the time, Pallas kernels for 11%

profile of v1, /device:TPU:17, one launch (start us, length us, event | category | flops | bytes accessed | tf_op | source)
XLA Modules:
  0.0 636.3 jit_solution(16411929714380311768)
XLA Ops:
  6.6 102.0 %while.11 = (s32[]{:T(128)}, s32[144,144]{1,0:T(8,128)}, s32[36,2]{0,1:T(2,128)S(1)}, s32[36,6]{1,0:T(8,128)S(1)}) while((s32[]{:T(128)}, s32[144,144]{1,0:T(8,128)}, s32[36,2]{0,1:T(2,128)S(1)}, s32[36,6]{1,0:T(8,128)S(1)}) %tuple.76), condition=%wide.while_cond.7.clone, body=%wide.while_body.7.sunk.clone | while | flops 2 | bytes 201 | solution.py:137
  7.2 2.1 dynamic-slice.89
  10.1 2.1 dynamic-slice.89
  12.9 2.1 dynamic-slice.89
  15.7 2.1 dynamic-slice.89
  18.6 2.1 dynamic-slice.89
  21.4 2.1 dynamic-slice.89
  24.2 2.1 dynamic-slice.89
  27.1 2.1 dynamic-slice.89
  29.9 2.1 dynamic-slice.89
  32.7 2.1 dynamic-slice.89
  35.6 2.1 dynamic-slice.89
  38.4 2.1 dynamic-slice.89
  41.2 2.1 dynamic-slice.89
  44.1 2.1 dynamic-slice.89
  46.9 2.1 dynamic-slice.89
  49.7 2.1 dynamic-slice.89
  52.6 2.1 dynamic-slice.89
  55.4 2.1 dynamic-slice.89
  58.2 2.1 dynamic-slice.89
  61.1 2.1 dynamic-slice.89
  63.9 2.1 dynamic-slice.89
  66.7 2.1 dynamic-slice.89
  69.6 2.1 dynamic-slice.89
  72.4 2.1 dynamic-slice.89
  75.2 2.1 dynamic-slice.89
  78.1 2.1 dynamic-slice.89
  80.9 2.1 dynamic-slice.89
  83.7 2.1 dynamic-slice.89
  86.6 2.1 dynamic-slice.89
  89.4 2.1 dynamic-slice.89
  92.2 2.1 dynamic-slice.89
  95.1 2.1 dynamic-slice.89
  97.9 2.1 dynamic-slice.89
  100.7 2.1 dynamic-slice.89
  103.6 2.1 dynamic-slice.89
  106.4 2.1 dynamic-slice.89
  110.6 2.4 constant_dynamic-slice_fusion.2
  113.1 3.0 fusion.3
  116.1 2.6 copy.63
  118.9 12.3 %fusion.1 = bf16[4,6,128,9,128]{2,1,4,3,0:T(8,128)(2,1)} fusion(bf16[4,9,6,128,128]{4,3,2,1,0:T(8,128)(2,1)} %bitcast.115, pred[4,9,6]{2,1,0:T(8,128)(4,1)S(1)} %reshape.408, pred[4,9]{1,0:T(4,128)(4,1)S(1)} %add_compare_fusion), kind=kLoop, calls=%fused_computation.4 | loop fusion | flops 7077888 | bytes 14156028 | tf_op jit(solution)/shard_map/transpose | solution.py:62
  131.2 15.4 %reshape.353 = bf16[4,768,1152]{1,2,0:T(8,128)(2,1)} reshape(bf16[4,6,128,9,128]{2,1,4,3,0:T(8,128)(2,1)} %fusion.1) | data formatting | bytes 14155776 | tf_op jit(solution)/shard_map/reshape | solution.py:63
  146.7 10.5 %copy.33.u_ref = bf16[4,768,1152]{2,1,0:T(8,128)(2,1)} copy(bf16[4,768,1152]{1,2,0:T(8,128)(2,1)} %reshape.353) | data formatting | bytes 14155776 | tf_op jit(solution)/shard_map/reshape | solution.py:63
  157.2 63.9 %shard_map.46 = (f32[36,18,128,128]{3,2,1,0:T(8,128)}, f32[2304,768]{1,0:T(8,128)}) custom-call(f32[36,18,128,128]{3,2,1,0:T(8,128)} %bitcast.125, bf16[4,768,1152]{2,1,0:T(8,128)(2,1)} %copy.33.u_ref), custom_call_target="tpu_custom_call" | custom-call | flops 32614907904 | bytes 84934656 | tf_op jit(solution)/shard_map/pallas_call | solution.py:64
  221.1 49.7 %while.12 = (s32[]{:T(128)}, s32[144,144]{1,0:T(8,128)}, s32[18,2]{0,1:T(2,128)S(1)}, s32[18,6]{1,0:T(8,128)S(1)}) while((s32[]{:T(128)}, s32[144,144]{1,0:T(8,128)}, s32[18,2]{0,1:T(2,128)S(1)}, s32[18,6]{1,0:T(8,128)S(1)}) %tuple.90), condition=%wide.while_cond.8.clone, body=%wide.while_body.8.sunk.clone | while | flops 2 | bytes 201 | solution.py:156
  227.3 2.1 dynamic-slice.91
  230.0 2.1 dynamic-slice.91
  260.4 2.1 dynamic-slice.91
  273.4 72.7 %reduce-scatter.3.cloned.1.call-done.y_ref = f32[576,768]{1,0:T(8,128)} async-done(((f32[2304,768]{1,0:T(8,128)}), f32[576,768]{1,0:T(8,128)}) %reduce-scatter.3.cloned.1.call-update) | async-done | bytes 1769488 | tf_op jit(solution)/shard_map/reduce_scatter | solution.py:154
  348.8 6.0 shard_map.47
  355.1 2.2 reshape.359
  357.3 3.6 copy.37
  360.8 3.6 all-to-all-start
  365.0 60.9 %all-to-all-done = f32[576,2,4,128]{3,0,1,2:T(8,128)S(1)} async-done(((f32[576,2,4,128]{3,0,1,2:T(8,128)}), f32[576,2,4,128]{3,0,1,2:T(8,128)S(1)}, u32[]{:S(2)}, u32[]{:S(2)}) %all-to-all-start) | async-done | bytes 2359328 | tf_op jit(solution)/shard_map/all_to_all | solution.py:180
  426.1 2.3 fusion.23
  429.7 6.0 collective-permute-start
  435.8 30.8 %copy.39 = f32[36,18,128,128]{3,2,0,1:T(8,128)} copy(f32[36,18,128,128]{3,2,1,0:T(8,128)} %get-tuple-element.93) | data formatting | bytes 84934656 | tf_op jit(solution)/shard_map/pallas_call | solution.py:64
  467.3 111.0 %all-reduce.5.cloned.1.call-done.p_ref = f32[768,768]{1,0:T(8,128)} async-done(((f32[768,768]{1,0:T(8,128)}), f32[768,768]{1,0:T(8,128)}) %all-reduce.5.cloned.1.call-update) | async-done | bytes 2359312 | tf_op jit(solution)/shard_map/psum | solution.py:168
  581.0 4.5 shard_map.48
  587.3 2.1 constant_dynamic-slice_fusion.4
  594.4 3.8 fusion.6
  598.3 2.4 fusion.16
  600.7 13.1 %copy.86 = f32[36,1,18,1,128,128]{5,4,2,0,3,1:T(8,128)S(1)} copy(f32[36,1,18,1,128,128]{5,4,2,0,3,1:T(8,128)} %bitcast.110) | data formatting | bytes 84934656
  615.2 14.6 %copy-done.4 = f32[36,1,18,1,128,128]{5,4,2,0,3,1:T(8,128)} copy-done((f32[36,1,18,1,128,128]{5,4,2,0,3,1:T(8,128)}, f32[36,1,18,1,128,128]{5,4,2,0,3,1:T(8,128)S(1)}, u32[]{:S(2)}) %copy-start.4) | copy-done | bytes 42467352
  (242 shorter events, 89.5 us)
Async XLA Ops:
  6.5 264.4 %all-gather.3.cloned.1.call-start = ((), (), s32[]{:S(2)}) async-start(), calls=%async_computation.6 | async-start | bytes 1966080 | tf_op jit(solution)/shard_map/all_gather | solution.py:143
  110.5 162.9 %reduce-scatter.5.cloned.1.call-start = ((), (), s32[]{:S(2)}) async-start(), calls=%async_computation.4 | async-start | bytes 4423680 | tf_op jit(solution)/shard_map/reduce_scatter | solution.py:152
  118.8 227.3 %reduce-scatter.3.cloned.1.call-start = ((), (), s32[]{:S(2)}) async-start(), calls=%async_computation.3 | async-start | bytes 8847360 | tf_op jit(solution)/shard_map/reduce_scatter | solution.py:154
  346.1 1.5 copy-start.1
  347.6 1.2 copy-start.2
  360.8 65.1 %all-to-all-start = ((f32[576,2,4,128]{3,0,1,2:T(8,128)}), f32[576,2,4,128]{3,0,1,2:T(8,128)S(1)}, u32[]{:S(2)}, u32[]{:S(2)}) async-start(f32[576,2,4,128]{3,0,1,2:T(8,128)} %copy.37), calls=%async_computation.2 | async-start | bytes 4718592 | tf_op jit(solution)/shard_map/all_to_all | solution.py:180
  364.4 213.9 %all-reduce.5.cloned.1.call-start = ((), (), s32[]{:S(2)}) async-start(), calls=%async_computation.5 | async-start | bytes 4718592 | tf_op jit(solution)/shard_map/psum | solution.py:168
  428.4 163.0 %collective-permute-start.1 = (f32[18,128,128]{2,1,0:T(8,128)}, f32[18,128,128]{2,1,0:T(8,128)}, u32[]{:S(2)}, u32[]{:S(2)}) collective-permute-start(f32[18,128,128]{2,1,0:T(8,128)} %get-tuple-element.137), channel_id=1, source_target_pairs={{4,0},{5,8},{6,16},{7,24},{12,1},{13,9},{14,17},{15,25},{20,2},{21... | collective-permute-start | bytes 3538952 | tf_op jit(solution)/shard_map/ppermute | solution.py:196
  429.7 161.8 %collective-permute-start = (f32[18,128,128]{2,1,0:T(8,128)}, f32[18,128,128]{2,1,0:T(8,128)}, u32[]{:S(2)}, u32[]{:S(2)}) collective-permute-start(f32[18,128,128]{2,1,0:T(8,128)} %get-tuple-element.138), channel_id=1, source_target_pairs={{0,0},{1,8},{2,16},{3,24},{8,1},{9,9},{10,17},{11,25},{16,2},{17,1... | collective-permute-start | bytes 3538952 | tf_op jit(solution)/shard_map/ppermute | solution.py:196
  578.4 1.7 copy-start
  580.0 1.0 copy-start.3
  587.3 3.7 copy-start.6
  593.5 0.8 copy-start.8
  593.5 0.9 copy-start.7
  594.4 3.9 copy-start.5
  615.2 14.6 %copy-start.4 = (f32[36,1,18,1,128,128]{5,4,2,0,3,1:T(8,128)}, f32[36,1,18,1,128,128]{5,4,2,0,3,1:T(8,128)S(1)}, u32[]{:S(2)}) copy-start(f32[36,1,18,1,128,128]{5,4,2,0,3,1:T(8,128)S(1)} %fusion.13) | copy-start | bytes 127401984
Sparse Core Ops, SparseCore 0:
  110.6 36.7 all-gather.2
  149.7 66.7 reduce-scatter.4
  221.2 124.9 reduce-scatter.2
  370.5 207.7 all-reduce.4

commit v2 on v1

v2 whole, which is shorter than its diff:
```python
import functools

import jax
import jax.numpy as jnp
from jax import lax
from jax.experimental import pallas as pl
from jax.experimental.pallas import tpu as pltpu
from jax.sharding import PartitionSpec as P

F32 = jnp.float32
BF16 = jnp.bfloat16


def largest_divisor(value, most):
    return max(d for d in range(1, most + 1) if value % d == 0)


def pieces(value, count):
    parts = []
    for _ in range(count):
        part = value.astype(BF16)
        parts.append(part)
        value = value - part.astype(F32)
    return parts


def mixed_dot(left, right, dims=(((1,), (0,)), ((), ())), count=3):
    total = None
    for part in reversed(pieces(left, count)):
        term = lax.dot_general(part, right, dims, preferred_element_type=F32)
        total = term if total is None else total + term
    return total


def turn_kernel(mask_ref, u_ref, t_ref):
    chunk = pl.program_id(0)
    tall, steps, width, _ = u_ref.shape
    for a in range(tall):
        for k in range(steps):
            row = chunk * tall + a
            block = jnp.where(mask_ref[row, k] > 0, u_ref[a, k].astype(F32), 0.0)
            t_ref[k * width : (k + 1) * width, a * width : (a + 1) * width] = block.T.astype(BF16)


def turned(lower, mask, tall):
    row_blocks, steps, width, _ = lower.shape
    chunks = row_blocks // tall
    return pl.pallas_call(
        turn_kernel,
        grid=(chunks,),
        in_specs=[
            pl.BlockSpec(memory_space=pltpu.SMEM),
            pl.BlockSpec((tall, steps, width, width), lambda k: (k, 0, 0, 0)),
        ],
        out_specs=pl.BlockSpec((None, steps * width, tall * width), lambda k: (k, 0, 0)),
        out_shape=jax.ShapeDtypeStruct((chunks, steps * width, tall * width), BF16),
        compiler_params=pltpu.CompilerParams(vmem_limit_bytes=40 << 20),
    )(mask, lower)


def product_kernel(x_ref, u_ref, *rest):
    o_ref, y_ref, acc_ref = rest[-3:]
    k = pl.program_id(1)
    tall, group, width, _ = x_ref.shape
    o_ref[...] = x_ref[...]
    tile = jnp.concatenate([x_ref[:, g].reshape(tall * width, width) for g in range(group)], axis=1)
    high, low = pieces(tile, 2)
    left = u_ref[k]
    part = jnp.dot(left, low, preferred_element_type=F32) + jnp.dot(left, high, preferred_element_type=F32)

    @pl.when(k == 0)
    def _():
        acc_ref[...] = part

    @pl.when(k > 0)
    def _():
        acc_ref[...] += part

    @pl.when(k == pl.num_programs(1) - 1)
    def _():
        y_ref[...] = acc_ref[...].T


def product(blocks, left, copied, start, count):
    row_blocks, _, width, _ = blocks.shape
    chunks, depth, length = left.shape
    group = 2 if count % 2 == 0 else 1
    tall = length // width
    place = pl.BlockSpec((tall, group, width, width), lambda c, k: (k, start // group + c, 0, 0))
    operands = [blocks, left]
    in_specs = [
        place,
        pl.BlockSpec(left.shape, lambda c, k: (0, 0, 0), pipeline_mode=pl.Buffered(1)),
    ]
    aliases = {}
    if copied is not None:
        operands.append(copied)
        in_specs.append(pl.BlockSpec(memory_space=pl.ANY))
        aliases = {2: 0}
    return pl.pallas_call(
        product_kernel,
        grid=(count // group, chunks),
        in_specs=in_specs,
        out_specs=[place, pl.BlockSpec((group * width, depth), lambda c, k: (c, 0))],
        out_shape=[
            jax.ShapeDtypeStruct(blocks.shape, F32),
            jax.ShapeDtypeStruct((count * width, depth), F32),
        ],
        scratch_shapes=[pltpu.VMEM((depth, group * width), F32)],
        input_output_aliases=aliases,
        compiler_params=pltpu.CompilerParams(vmem_limit_bytes=56 << 20),
        cost_estimate=pl.CostEstimate(
            flops=4 * row_blocks * count * width**2 * depth,
            bytes_accessed=8 * row_blocks * count * width**2,
            transcendentals=0,
        ),
    )(*operands)


def write_kernel(flag_ref, col_ref, row_ref, x_ref, o_ref, sem):
    slots = row_ref.shape[0]

    @pl.when(flag_ref[0] > 0)
    def _():
        copy = pltpu.make_async_copy(col_ref, o_ref.at[:, 0], sem.at[0])
        copy.start()
        copy.wait()

    for slot in range(slots):

        @pl.when(flag_ref[1 + slot] > 0)
        def _():
            copy = pltpu.make_async_copy(row_ref.at[slot], o_ref.at[slot], sem.at[1 + slot])
            copy.start()
            copy.wait()


def write(flags, new_col, new_rows, copied):
    slots = new_rows.shape[0]
    return pl.pallas_call(
        write_kernel,
        in_specs=[
            pl.BlockSpec(memory_space=pltpu.SMEM),
            pl.BlockSpec(memory_space=pltpu.VMEM),
            pl.BlockSpec(memory_space=pltpu.VMEM),
            pl.BlockSpec(memory_space=pl.ANY),
        ],
        out_specs=pl.BlockSpec(memory_space=pl.ANY),
        out_shape=jax.ShapeDtypeStruct(copied.shape, F32),
        scratch_shapes=[pltpu.SemaphoreType.DMA((1 + slots,))],
        input_output_aliases={3: 0},
        compiler_params=pltpu.CompilerParams(vmem_limit_bytes=40 << 20),
    )(flags, new_col, new_rows, copied)


def packed(j, k):
    return j * (j + 1) // 2 + k


def substitute_kernel(steps, y_ref, mask_ref, small_ref, rows_ref, z_ref, p_ref):
    width = y_ref.shape[1] // steps
    for k in reversed(range(steps)):
        here = slice(k * width, (k + 1) * width)
        value = y_ref[:, here]
        if k + 1 < steps:
            later = slice((k + 1) * width, steps * width)
            value = value + mixed_dot(z_ref[:, later], small_ref[later, here])
        z_ref[:, here] = jnp.where(mask_ref[:, k : k + 1] > 0, -value, 0.0)
    for j in range(steps):
        upto = slice(0, (j + 1) * width)
        there = slice(j * width, (j + 1) * width)
        value = mixed_dot(z_ref[:, there], rows_ref[:, upto], (((0,), (0,)), ((), ())))
        for k in range(j + 1):
            p_ref[packed(j, k)] = value[:, k * width : (k + 1) * width]


def corner_kernel(steps, p_ref, small_ref, dinv_ref, mask_ref, s_ref):
    width = dinv_ref.shape[1]
    for k in reversed(range(steps)):
        here = slice(k * width, (k + 1) * width)
        diag = dinv_ref[k] - p_ref[packed(k, k)].T
        if k + 1 < steps:
            later = slice((k + 1) * width, steps * width)
            factor = small_ref[later, here]
            known = jnp.concatenate([p_ref[packed(j, k)] for j in range(k + 1, steps)], axis=0)
            value = known + mixed_dot(s_ref[later, later], factor)
            value = jnp.where(mask_ref[later, k : k + 1] > 0, -value, 0.0)
            diag = diag - mixed_dot(value, factor, (((0,), (0,)), ((), ()))).T
            s_ref[later, here] = value
            s_ref[here, later] = value.T
        s_ref[here, here] = diag.T


def per_device(ainv_in, ufactor, dinv, pattern):
    row_blocks, _, col_blocks, _, width, _ = ainv_in.shape
    steps = dinv.shape[0]
    blocks = ainv_in.reshape(row_blocks, col_blocks, width, width)
    lower = ufactor.reshape(row_blocks, steps, width, width)
    row_count = lax.axis_size("prow")
    col_count = lax.axis_size("pcol")
    prow_id = lax.axis_index("prow")
    pcol_id = lax.axis_index("pcol")
    fold = col_count // row_count
    slots = -(-steps // row_count)
    assert slots <= fold and steps <= col_count
    row_ids = jnp.arange(row_blocks, dtype=jnp.int32) * row_count + prow_id
    col_ids = jnp.arange(col_blocks, dtype=jnp.int32) * col_count + pcol_id

    heads = pattern[:, :steps]
    row_pattern = lax.dynamic_index_in_dim(heads.reshape(row_blocks, row_count, steps), prow_id, 1, keepdims=False)
    col_pattern = lax.dynamic_index_in_dim(heads.reshape(col_blocks, col_count, steps), pcol_id, 1, keepdims=False)
    outer_rows = jnp.where((row_ids >= steps)[:, None], row_pattern, 0)
    outer_cols = jnp.where((col_ids >= steps)[:, None], col_pattern, 0)

    heads_live = row_pattern[:slots] > 0
    small = jnp.where(heads_live[:, :, None, None], lower[:slots], jnp.zeros_like(lower[:slots]))
    small = lax.all_gather(small, "prow", axis=1)
    small = small.reshape(slots * row_count, steps, width, width)[:steps]
    small = small.transpose(0, 2, 1, 3).reshape(steps * width, steps * width)

    chosen = lax.dynamic_index_in_dim(
        lower.reshape(col_blocks, fold, steps, width, width), pcol_id // row_count, 1, keepdims=False
    )
    at_home = (outer_cols > 0) & (prow_id == pcol_id % row_count)
    chosen = jnp.where(at_home[:, :, None, None], chosen, jnp.zeros_like(chosen))
    chosen = chosen.transpose(0, 2, 1, 3).reshape(col_blocks * width, steps * width)

    left = turned(lower, outer_rows, largest_divisor(row_blocks, 9))
    parts = 3 if col_blocks % 3 == 0 else 1
    count = col_blocks // parts
    span = count * width
    share = span // row_count
    mask_all = jnp.repeat(outer_cols.astype(F32), width, axis=0)
    params = pltpu.CompilerParams(vmem_limit_bytes=40 << 20)
    triangle = steps * (steps + 1) // 2
    copied, products, mine_parts, received_parts = None, None, [], []
    for part in range(parts):
        copied, partial_y = product(blocks, left, copied, part * count, count)
        here = slice(part * span, (part + 1) * span)
        factor_rows = lax.psum_scatter(chosen[here], "prow", scatter_dimension=0, tiled=True)
        share_y = lax.psum_scatter(partial_y, "prow", scatter_dimension=0, tiled=True)
        mask_rows = lax.dynamic_slice_in_dim(mask_all[here], prow_id * share, share, 0)
        share_z, product_part = pl.pallas_call(
            functools.partial(substitute_kernel, steps),
            out_shape=[
                jax.ShapeDtypeStruct(share_y.shape, F32),
                jax.ShapeDtypeStruct((triangle, width, width), F32),
            ],
            compiler_params=params,
        )(share_y, mask_rows, small, factor_rows)
        products = product_part if products is None else products + product_part

        padded = jnp.pad(share_z, ((0, 0), (0, (slots * row_count - steps) * width)))
        padded = padded.reshape(share, slots, row_count, width)
        mine = lax.all_to_all(padded, "prow", split_axis=2, concat_axis=0, tiled=True)
        mine = mine.reshape(count, width, slots, width)
        mine_parts.append(mine)

        received = []
        for turn in range(fold):
            pairs = []
            for slot in range(slots):
                side = (turn + slot) % fold
                for p in range(row_count):
                    if slot * row_count + p < steps:
                        for r in range(row_count):
                            source = p * col_count + side * row_count + r
                            target = r * col_count + slot * row_count + p
                            pairs.append((source, target))
            slot = jnp.minimum((pcol_id // row_count + fold - turn) % fold, slots - 1)
            payload = lax.dynamic_index_in_dim(mine, slot, 2, keepdims=False)
            received.append(lax.ppermute(payload, ("prow", "pcol"), pairs))
        received_parts.append(jnp.stack(received))
    products = lax.psum(products, ("prow", "pcol"))
    mine = jnp.concatenate(mine_parts, axis=0)
    stacked = jnp.concatenate(received_parts, axis=1)

    mask_small = jnp.repeat(pattern[:steps, :steps].astype(F32), width, axis=0)
    corner = pl.pallas_call(
        functools.partial(corner_kernel, steps),
        out_shape=jax.ShapeDtypeStruct((steps * width, steps * width), F32),
        compiler_params=params,
    )(products, small, dinv, mask_small)
    corner = corner.reshape(steps, width, steps, width)

    my_slot = pcol_id // row_count
    new_col = jnp.stack([stacked[(side - my_slot) % fold] for side in range(fold)], axis=1)
    new_col = new_col.reshape(row_blocks, width, width)
    own = jnp.minimum(pcol_id, steps - 1)
    corner_col = lax.dynamic_index_in_dim(corner, own, 2, keepdims=False)
    for slot in range(slots):
        index = slot * row_count + prow_id
        block = lax.dynamic_index_in_dim(corner_col, jnp.minimum(index, steps - 1), 0, keepdims=False)
        new_col = new_col.at[slot].set(jnp.where(index < steps, block, new_col[slot]))
    new_rows, flags = [], [pcol_id < steps]
    for slot in range(slots):
        index = slot * row_count + prow_id
        new_row = jnp.swapaxes(mine[:, :, slot], 1, 2)
        block = lax.dynamic_index_in_dim(corner, jnp.minimum(index, steps - 1), 0, keepdims=False)
        block = lax.dynamic_index_in_dim(block, own, 1, keepdims=False)
        new_rows.append(new_row.at[0].set(jnp.where(pcol_id < steps, block, new_row[0])))
        flags.append(index < steps)
    matrix = write(jnp.stack(flags).astype(jnp.int32), new_col, jnp.stack(new_rows), copied)
    return matrix.reshape(ainv_in.shape)


def solution(mesh):
    placed = (
        P(None, "prow", None, "pcol", None, None),
        P(None, "prow", None, None, None),
        P(),
        P(),
    )
    return jax.shard_map(
        per_device,
        mesh=mesh,
        in_specs=placed,
        out_specs=P(None, "prow", None, "pcol", None, None),
        check_vma=False,
    )
```

time: 647 us -> 626 us (0.968); the launches traced: 636 us -> 624 us
  local copies, waits for them, and re-layouts: 264 us -> 53.9 us
  waiting for transfers between devices: 245 us -> 426 us
  starting transfers between devices: 11.1 us -> 32.1 us
  other arithmetic: 28 us -> 9.17 us
  Pallas kernels: 74.3 us -> 88.9 us
    gather x216 -> x0, local copies, waits for them, and re-layouts: 151 us -> none
    ppermute x2 -> x6, waiting for transfers between devices: 0.01 us -> 88.5 us  [per_device(): received.append(lax.ppermute(payload, ('prow', 'pcol'), pairs))]
    reduce_scatter x1 -> x3, waiting for transfers between devices: 72.7 us -> 142 us  [per_device(): lax.psum_scatter(partial_y, 'prow', scatter_dimension=0, tiled=True)]
    all_to_all x1 -> x3, waiting for transfers between devices: 60.9 us -> 0.01 us  [per_device(): lax.all_to_all(padded, 'prow', split_axis=2, concat_axis=0, tiled=True)]
    reduce_scatter x1 -> x3, waiting for transfers between devices: 0.02 us -> 59.4 us  [per_device(): lax.psum_scatter(chosen[here], 'prow', scatter_dimension=0, tiled=True)]
    pallas_call x1 -> x0, local copies, waits for them, and re-layouts: 30.8 us -> none  [product(): pl.pallas_call(product_kernel, grid=(col_blocks // group, chunks), in_spe...]
    reshape x2 -> x4, local copies, waits for them, and re-layouts: 25.9 us -> 1.68 us  [the longest x1 0.89 us: per_device(): heads.reshape(col_blocks, col_count, steps)]
    psum x1, waiting for transfers between devices: 111 us -> 135 us  [per_device(): products = lax.psum(products, ('prow', 'pcol'))]
  transfers between devices with their start and end apart: 7 -> 17, of which waited for: 3 -> 12; matrix products, arithmetic and copies ran while one was open for 22% -> 6% of each run, Pallas kernels for 11% -> 14%
where the time goes in v2:
time: 626 us; the launch traced here: 624 us
  waiting for transfers between devices  426 us (68%)
  Pallas kernels  88.9 us (14%)
  local copies, waits for them, and re-layouts  53.9 us (9%)
  starting transfers between devices  32.1 us (5%)
  between operations  14.1 us (2%)
  other arithmetic  9.17 us (1%)
    reduce_scatter x3, waiting for transfers between devices, per_device(): lax.psum_scatter(partial_y, 'prow', scatter_dimension=0, tiled=True)  142 us
    psum x1, waiting for transfers between devices, per_device(): products = lax.psum(products, ('prow', 'pcol'))  135 us
    ppermute x6, waiting for transfers between devices, per_device(): received.append(lax.ppermute(payload, ('prow', 'pcol'), pairs))  88.5 us
    pallas_call x3, Pallas kernels, product(): pl.pallas_call(product_kernel, grid=(count // group, chunks), in_specs=in...  72 us
    reduce_scatter x3, waiting for transfers between devices, per_device(): lax.psum_scatter(chosen[here], 'prow', scatter_dimension=0, tiled=True)  59.4 us
    unnamed x35, local copies, waits for them, and re-layouts  21.6 us
    ppermute x6, starting transfers between devices, per_device(): received.append(lax.ppermute(payload, ('prow', 'pcol'), pairs))  18.4 us
    all_to_all x3, starting transfers between devices, per_device(): lax.all_to_all(padded, 'prow', split_axis=2, concat_axis=0, tiled=True)  13.3 us
  transfers between devices with their start and end apart: 17, of which 12 were waited for; matrix products, arithmetic and copies ran while one was open for 6% of the time, Pallas kernels for 14%

profile of v2, /device:TPU:17, one launch (start us, length us, event | category | flops | bytes accessed | tf_op | source)
XLA Modules:
  0.0 623.8 jit_solution(11616158576783184731)
XLA Ops:
  7.5 1.8 slice_select_fusion
  9.7 2.4 constant_dynamic-slice_fusion.4
  12.1 2.4 fusion
  15.4 1.2 copy.84
  16.8 3.3 copy-done.1
  20.1 3.3 shard_map.46.u_ref
  23.4 2.9 copy-done
  26.3 24.0 %shard_map.47 = (f32[36,18,128,128]{3,2,1,0:T(8,128)}, f32[768,768]{1,0:T(8,128)}) custom-call(f32[36,18,128,128]{3,2,1,0:T(8,128)} %bitcast.127, bf16[4,768,1152]{2,1,0:T(8,128)(2,1)} %copy-done), custom_call_target="tpu_custom_call" | custom-call | flops 10871635968 | bytes 28311552 | tf_op jit(solution)/shard_map/pallas_call | solution.py:100
  50.3 24.0 %shard_map.49 = (f32[36,18,128,128]{3,2,1,0:T(8,128)}, f32[768,768]{1,0:T(8,128)}) custom-call(f32[36,18,128,128]{3,2,1,0:T(8,128)} %bitcast.128, bf16[4,768,1152]{2,1,0:T(8,128)(2,1)} %copy-done, f32[36,18,128,128]{3,2,1,0:T(8,128)} %get-tuple-element.67.rest_0_), custom_call_target="tpu_custom_call", output_to_operand_aliasing={{0}: (2, {})} | custom-call | flops 10871635968 | bytes 28311552 | tf_op jit(solution)/shard_map/pallas_call | solution.py:100
  74.3 24.0 %shard_map.51 = (f32[36,18,128,128]{3,2,1,0:T(8,128)}, f32[768,768]{1,0:T(8,128)}) custom-call(f32[36,18,128,128]{3,2,1,0:T(8,128)} %bitcast.129, bf16[4,768,1152]{2,1,0:T(8,128)(2,1)} %copy-done, f32[36,18,128,128]{3,2,1,0:T(8,128)} %get-tuple-element.70.rest_0_), custom_call_target="tpu_custom_call", output_to_operand_aliasing={{0}: (2, {})} | custom-call | flops 10871635968 | bytes 28311552 | tf_op jit(solution)/shard_map/pallas_call | solution.py:100
  98.4 1.2 copy.85
  100.3 1.2 copy.86
  102.6 1.3 slice.178
  105.0 41.6 %reduce-scatter.15.cloned.1.call-done.y_ref = f32[192,768]{1,0:T(8,128)} async-done(((f32[768,768]{1,0:T(8,128)}), f32[192,768]{1,0:T(8,128)}) %reduce-scatter.15.cloned.1.call-update) | async-done | bytes 589840 | tf_op jit(solution)/shard_map/reduce_scatter | solution.py:241
  146.6 1.1 copy-done.7
  147.6 1.0 copy-done.10
  148.6 2.0 shard_map.52
  150.7 1.2 reshape.265
  152.0 2.2 copy.62
  154.2 4.0 all-to-all-start.2
  158.3 32.6 %reduce-scatter.13.cloned.1.call-done.rows_ref = bf16[192,768]{1,0:T(8,128)(2,1)} async-done(((bf16[768,768]{1,0:T(8,128)(2,1)}), bf16[192,768]{1,0:T(8,128)(2,1)}) %reduce-scatter.13.cloned.1.call-update) | async-done | bytes 294928 | tf_op jit(solution)/shard_map/reduce_scatter | solution.py:240
  190.9 50.0 %reduce-scatter.11.cloned.1.call-done.y_ref = f32[192,768]{1,0:T(8,128)} async-done(((f32[768,768]{1,0:T(8,128)}), f32[192,768]{1,0:T(8,128)}) %reduce-scatter.11.cloned.1.call-update) | async-done | bytes 589840 | tf_op jit(solution)/shard_map/reduce_scatter | solution.py:241
  240.9 1.1 copy-done.6
  241.9 1.0 copy-done.11
  242.9 2.0 shard_map.50
  245.0 1.1 copy-done.3
  246.1 1.0 pad.19
  247.1 2.4 reshape.263
  249.5 2.2 copy.59
  251.7 4.6 all-to-all-start.1
  256.5 26.8 %reduce-scatter.9.cloned.1.call-done.rows_ref = bf16[192,768]{1,0:T(8,128)(2,1)} async-done(((bf16[768,768]{1,0:T(8,128)(2,1)}), bf16[192,768]{1,0:T(8,128)(2,1)}) %reduce-scatter.9.cloned.1.call-update) | async-done | bytes 294928 | tf_op jit(solution)/shard_map/reduce_scatter | solution.py:240
  283.2 50.1 %reduce-scatter.7.cloned.1.call-done.y_ref = f32[192,768]{1,0:T(8,128)} async-done(((f32[768,768]{1,0:T(8,128)}), f32[192,768]{1,0:T(8,128)}) %reduce-scatter.7.cloned.1.call-update) | async-done | bytes 589840 | tf_op jit(solution)/shard_map/reduce_scatter | solution.py:241
  333.3 1.1 copy-done.5
  334.4 1.0 copy-done.9
  335.4 2.0 shard_map.48
  337.4 1.1 copy-done.4
  338.5 1.0 pad.18
  339.5 2.4 reshape.261
  341.8 2.2 copy.56
  344.0 4.7 all-to-all-start
  348.7 3.1 add_add_fusion
  352.7 135.0 %all-reduce.5.cloned.1.call-done.p_ref = f32[21,128,128]{2,1,0:T(8,128)} async-done(((f32[21,128,128]{2,1,0:T(8,128)}), f32[21,128,128]{2,1,0:T(8,128)}) %all-reduce.5.cloned.1.call-update) | async-done | bytes 1376272 | tf_op jit(solution)/shard_map/psum | solution.py:274
  487.7 1.3 copy-done.2
  489.0 1.0 copy-done.8
  490.0 4.5 shard_map.53
  494.5 1.8 reshape.269
  496.3 1.3 constant_dynamic-slice_fusion
  497.7 1.2 copy.63
  499.1 1.2 copy.60
  501.5 1.0 dynamic-slice_bitcast_fusion.5
  502.5 1.2 copy.57
  504.9 1.3 collective-permute-start.5
  506.2 6.6 %collective-permute-start.4 = (f32[6,128,128]{2,1,0:T(8,128)}, f32[6,128,128]{2,1,0:T(8,128)S(1)}, u32[]{:S(2)}, u32[]{:S(2)}) collective-permute-start(f32[6,128,128]{2,1,0:T(8,128)} %get-tuple-element.92), channel_id=1, source_target_pairs={{0,0},{1,8},{2,16},{3,24},{8,1},{9,9},{10,17},{11,25},{16,2},{17,1... | collective-permute-start | bytes 1179656 | tf_op jit(solution)/shard_map/ppermute | solution.py:272
  512.9 1.3 collective-permute-start.3
  514.2 5.4 collective-permute-start.2
  519.6 1.3 collective-permute-start.1
  521.8 49.0 %collective-permute-done.5 = f32[6,128,128]{2,1,0:T(8,128)S(1)} collective-permute-done((f32[6,128,128]{2,1,0:T(8,128)}, f32[6,128,128]{2,1,0:T(8,128)S(1)}, u32[]{:S(2)}, u32[]{:S(2)}) %collective-permute-start.5) | collective-permute-done | bytes 393248 | tf_op jit(solution)/shard_map/ppermute | solution.py:272
  570.8 2.4 collective-permute-start
  573.4 6.4 %collective-permute-done.4 = f32[6,128,128]{2,1,0:T(8,128)S(1)} collective-permute-done((f32[6,128,128]{2,1,0:T(8,128)}, f32[6,128,128]{2,1,0:T(8,128)S(1)}, u32[]{:S(2)}, u32[]{:S(2)}) %collective-permute-start.4) | collective-permute-done | bytes 393248 | tf_op jit(solution)/shard_map/ppermute | solution.py:272
  579.8 7.9 %collective-permute-done.3 = f32[6,128,128]{2,1,0:T(8,128)S(1)} collective-permute-done((f32[6,128,128]{2,1,0:T(8,128)}, f32[6,128,128]{2,1,0:T(8,128)S(1)}, u32[]{:S(2)}, u32[]{:S(2)}) %collective-permute-start.3) | collective-permute-done | bytes 393248 | tf_op jit(solution)/shard_map/ppermute | solution.py:272
  587.7 9.0 %collective-permute-done.2 = f32[6,128,128]{2,1,0:T(8,128)S(1)} collective-permute-done((f32[6,128,128]{2,1,0:T(8,128)}, f32[6,128,128]{2,1,0:T(8,128)S(1)}, u32[]{:S(2)}, u32[]{:S(2)}) %collective-permute-start.2) | collective-permute-done | bytes 393248 | tf_op jit(solution)/shard_map/ppermute | solution.py:272
  596.6 7.9 %collective-permute-done.1 = f32[6,128,128]{2,1,0:T(8,128)S(1)} collective-permute-done((f32[6,128,128]{2,1,0:T(8,128)}, f32[6,128,128]{2,1,0:T(8,128)S(1)}, u32[]{:S(2)}, u32[]{:S(2)}) %collective-permute-start.1) | collective-permute-done | bytes 393248 | tf_op jit(solution)/shard_map/ppermute | solution.py:272
  604.5 8.4 %collective-permute-done = f32[6,128,128]{2,1,0:T(8,128)S(1)} collective-permute-done((f32[6,128,128]{2,1,0:T(8,128)S(1)}, f32[6,128,128]{2,1,0:T(8,128)S(1)}, u32[]{:S(2)}, u32[]{:S(2)}) %collective-permute-start) | collective-permute-done | bytes 393248 | tf_op jit(solution)/shard_map/ppermute | solution.py:272
  613.9 3.0 shard_map.54
  (81 shorter events, 10.8 us)
Async XLA Ops:
  6.5 96.0 %all-gather.2.cloned.1.call-start = ((), (), s32[]{:S(2)}) async-start(), calls=%async_computation.10 | async-start | bytes 1966080 | tf_op jit(solution)/shard_map/all_gather | solution.py:217
  9.3 95.7 %reduce-scatter.17.cloned.1.call-start = ((), (), s32[]{:S(2)}) async-start(), calls=%async_computation.15 | async-start | bytes 1474560 | tf_op jit(solution)/shard_map/reduce_scatter | solution.py:240
  16.6 129.9 %reduce-scatter.15.cloned.1.call-start = ((), (), s32[]{:S(2)}) async-start(), calls=%async_computation.14 | async-start | bytes 2949120 | tf_op jit(solution)/shard_map/reduce_scatter | solution.py:241
  16.8 3.3 copy-start.1
  23.4 2.9 copy-start
  98.3 92.6 %reduce-scatter.13.cloned.1.call-start = ((), (), s32[]{:S(2)}) async-start(), calls=%async_computation.13 | async-start | bytes 1474560 | tf_op jit(solution)/shard_map/reduce_scatter | solution.py:240
  99.7 141.2 %reduce-scatter.11.cloned.1.call-start = ((), (), s32[]{:S(2)}) async-start(), calls=%async_computation.12 | async-start | bytes 2949120 | tf_op jit(solution)/shard_map/reduce_scatter | solution.py:241
  100.2 183.0 %reduce-scatter.9.cloned.1.call-start = ((), (), s32[]{:S(2)}) async-start(), calls=%async_computation.11 | async-start | bytes 1474560 | tf_op jit(solution)/shard_map/reduce_scatter | solution.py:240
  101.6 231.8 %reduce-scatter.7.cloned.1.call-start = ((), (), s32[]{:S(2)}) async-start(), calls=%async_computation.9 | async-start | bytes 2949120 | tf_op jit(solution)/shard_map/reduce_scatter | solution.py:241
  146.6 1.1 copy-start.7
  147.6 1.0 copy-start.10
  154.2 97.5 %all-to-all-start.2 = ((f32[192,2,4,128]{3,0,1,2:T(8,128)}), f32[192,2,4,128]{3,0,1,2:T(8,128)S(1)}, u32[]{:S(2)}, u32[]{:S(2)}) async-start(f32[192,2,4,128]{3,0,1,2:T(8,128)} %copy.62), calls=%async_computation.8 | async-start | bytes 1572864 | tf_op jit(solution)/shard_map/all_to_all | solution.py:255
  240.9 1.1 copy-start.6
  241.9 1.0 copy-start.11
  244.9 1.1 copy-start.3
  251.7 87.8 %copy-start.12 = (f32[192,2,4,128]{3,0,1,2:T(8,128)}, f32[192,2,4,128]{3,0,1,2:T(8,128)S(1)}, u32[]{:S(2)}) copy-start(f32[192,2,4,128]{3,0,1,2:T(8,128)S(1)} %all-to-all-done.2) | copy-start | bytes 2359300
  251.7 92.3 %all-to-all-start.1 = ((f32[192,2,4,128]{3,0,1,2:T(8,128)}), f32[192,2,4,128]{3,0,1,2:T(8,128)}, u32[]{:S(2)}, u32[]{:S(2)}) async-start(f32[192,2,4,128]{3,0,1,2:T(8,128)} %copy.59), calls=%async_computation.5 | async-start | bytes 1572864 | tf_op jit(solution)/shard_map/all_to_all | solution.py:255
  333.3 1.1 copy-start.5
  334.4 1.0 copy-start.9
  337.4 1.1 copy-start.4
  344.0 158.5 %all-to-all-start = ((f32[192,2,4,128]{3,0,1,2:T(8,128)}), f32[192,2,4,128]{3,0,1,2:T(8,128)}, u32[]{:S(2)}, u32[]{:S(2)}) async-start(f32[192,2,4,128]{3,0,1,2:T(8,128)} %copy.56), calls=%async_computation.2 | async-start | bytes 1572864 | tf_op jit(solution)/shard_map/all_to_all | solution.py:255
  348.7 139.0 %all-reduce.5.cloned.1.call-start = ((), (), s32[]{:S(2)}) async-start(), calls=%async_computation.16 | async-start | bytes 2752512 | tf_op jit(solution)/shard_map/psum | solution.py:274
  487.7 1.3 copy-start.2
  489.0 1.0 copy-start.8
  504.9 65.9 %collective-permute-start.5 = (f32[6,128,128]{2,1,0:T(8,128)}, f32[6,128,128]{2,1,0:T(8,128)S(1)}, u32[]{:S(2)}, u32[]{:S(2)}) collective-permute-start(f32[6,128,128]{2,1,0:T(8,128)} %get-tuple-element.93), channel_id=1, source_target_pairs={{4,0},{5,8},{6,16},{7,24},{12,1},{13,9},{14,17},{15,25},{20,2},{21... | collective-permute-start | bytes 1179656 | tf_op jit(solution)/shard_map/ppermute | solution.py:272
  506.2 73.6 %collective-permute-start.4 = (f32[6,128,128]{2,1,0:T(8,128)}, f32[6,128,128]{2,1,0:T(8,128)S(1)}, u32[]{:S(2)}, u32[]{:S(2)}) collective-permute-start(f32[6,128,128]{2,1,0:T(8,128)} %get-tuple-element.92), channel_id=1, source_target_pairs={{0,0},{1,8},{2,16},{3,24},{8,1},{9,9},{10,17},{11,25},{16,2},{17,1... | collective-permute-start | bytes 1179656 | tf_op jit(solution)/shard_map/ppermute | solution.py:272
  512.9 74.8 %collective-permute-start.3 = (f32[6,128,128]{2,1,0:T(8,128)}, f32[6,128,128]{2,1,0:T(8,128)S(1)}, u32[]{:S(2)}, u32[]{:S(2)}) collective-permute-start(f32[6,128,128]{2,1,0:T(8,128)} %get-tuple-element.91), channel_id=1, source_target_pairs={{4,0},{5,8},{6,16},{7,24},{12,1},{13,9},{14,17},{15,25},{20,2},{21... | collective-permute-start | bytes 1179656 | tf_op jit(solution)/shard_map/ppermute | solution.py:272
  514.2 82.5 %collective-permute-start.2 = (f32[6,128,128]{2,1,0:T(8,128)}, f32[6,128,128]{2,1,0:T(8,128)S(1)}, u32[]{:S(2)}, u32[]{:S(2)}) collective-permute-start(f32[6,128,128]{2,1,0:T(8,128)} %get-tuple-element.90), channel_id=1, source_target_pairs={{0,0},{1,8},{2,16},{3,24},{8,1},{9,9},{10,17},{11,25},{16,2},{17,1... | collective-permute-start | bytes 1179656 | tf_op jit(solution)/shard_map/ppermute | solution.py:272
  519.6 84.9 %collective-permute-start.1 = (f32[6,128,128]{2,1,0:T(8,128)}, f32[6,128,128]{2,1,0:T(8,128)S(1)}, u32[]{:S(2)}, u32[]{:S(2)}) collective-permute-start(f32[6,128,128]{2,1,0:T(8,128)} %get-tuple-element.89), channel_id=1, source_target_pairs={{4,0},{5,8},{6,16},{7,24},{12,1},{13,9},{14,17},{15,25},{20,2},{21... | collective-permute-start | bytes 1179656 | tf_op jit(solution)/shard_map/ppermute | solution.py:272
  521.2 49.6 %copy-start.13 = (f32[6,128,128]{2,1,0:T(8,128)S(1)}, f32[6,128,128]{2,1,0:T(8,128)}, u32[]{:S(2)}) copy-start(f32[6,128,128]{2,1,0:T(8,128)} %get-tuple-element.88) | copy-start | bytes 1179652
  570.8 42.1 %collective-permute-start = (f32[6,128,128]{2,1,0:T(8,128)S(1)}, f32[6,128,128]{2,1,0:T(8,128)S(1)}, u32[]{:S(2)}, u32[]{:S(2)}) collective-permute-start(f32[6,128,128]{2,1,0:T(8,128)S(1)} %copy-done.13), channel_id=1, source_target_pairs={{0,0},{1,8},{2,16},{3,24},{8,1},{9,9},{10,17},{11,25},{16,2},{17,1... | collective-permute-start | bytes 1179656 | tf_op jit(solution)/shard_map/ppermute | solution.py:272
Sparse Core Ops, SparseCore 0:
  9.5 36.7 all-gather.1
  48.6 28.0 reduce-scatter.16
  98.5 48.0 reduce-scatter.14
  148.8 42.1 reduce-scatter.12
  193.1 47.7 reduce-scatter.10
  243.0 40.1 reduce-scatter.8
  285.5 47.7 reduce-scatter.6
  354.8 132.7 all-reduce.4
